TPU v7x, 128 devices: a whole 4x4x4 slice. The times are simulated.
128 devices in a mesh: slab: 16 (over z, x), pencil: 8 (over y, core).
Axes of the slice: x: 4, y: 4, z: 4, core: 2. Of those that a mesh axis runs over, the one named last changes fastest.
Arguments:
- a_blocks: float32 [256, 64, 20480], P('slab', 'pencil'), may hold values from -1 to 8, as said below
- col_codes: int32 [256, 64, 5], P('slab', 'pencil'), may hold values from 0 to 8, as said below
- agg_of: int32 [256, 64], P('slab', 'pencil'), may hold values from 0 to 2047, as said below
- test_vectors: float32 [256, 64, 2048], P('slab', 'pencil'), may hold values from -36 to 36
Outputs:
- relaxed: float32 [256, 64, 2048], P('slab', 'pencil')
- tiles: float32 [256, 64, 512], P('slab', 'pencil')
- products: float32 [256, 64, 2560], P('slab', 'pencil')
Inputs may be any that keep to these rules, and one draw needn't show every extreme that they name: `col_codes`: slot 0 of every block row is code 4, the block row itself; slots 1 to 4 hold different codes among the other eight of the 3 x 3 neighbourhood. `agg_of`: aggregate g is owned by device g // 16, devices numbered slab-major. On each device the block rows, in row-major order, form 64 groups of 2 consecutive block rows; all block rows of a group belong to aggregates of one owner, and the groups of one device go to different owners. Some owners receive a group from every device. `a_blocks`: the diagonal entries of every slot-0 block lie in [1.99, 8].
All inputs are finite; a program needn't handle non-finite values.
Results may differ from a plain program's by a relative error of at most 0.0003.
Values sent between devices are 32-bit elements; how exact they have to be, the bound alone decides.
A program may use at most 320 MiB of HBM per device.

v0:
```python
import math
import jax
import jax.numpy as jnp
from jax import lax
from jax.sharding import PartitionSpec as P

BLK = 64
NV = 32
NC = 8
KS = 5
ITERS = 2
OMEGA = 2.0 / 3.0
FULL_PRECISION = lax.Precision.HIGHEST


def with_halo(cells, sides, width):
    for axis, dim in sides:
        count = lax.axis_size(axis)
        ends = count - 1
        head = lax.slice_in_dim(cells, 0, width, axis=dim)
        tail = lax.slice_in_dim(cells, cells.shape[dim] - width, cells.shape[dim], axis=dim)
        cells = jnp.concatenate(
            [
                lax.ppermute(tail, axis, [(i, (i + 1) % count) for i in range(ends)]),
                cells,
                lax.ppermute(head, axis, [((i + 1) % count, i) for i in range(ends)]),
            ],
            axis=dim,
        )
    return cells


def coarse_modes(cells, coarse):
    centre = jnp.arange(cells, dtype=jnp.float32) + 0.5
    order = jnp.arange(coarse, dtype=jnp.float32)
    return jnp.cos(math.pi * centre[:, None] * order[None, :] / cells)


def solve_maps(coarse):
    gram = jnp.einsum("gkv,glv->gkl", coarse, coarse, precision=FULL_PRECISION)
    trace_sum = jnp.trace(gram, axis1=1, axis2=2)
    ridge = 0.1 * trace_sum / NC + 1e-06
    gram = gram + ridge[:, None, None] * jnp.eye(NC, dtype=jnp.float32)[None]
    lower = jnp.linalg.cholesky(gram)
    half_solved = jax.scipy.linalg.solve_triangular(lower, coarse, lower=True)
    solved = jax.scipy.linalg.solve_triangular(lower, half_solved, lower=True, trans=1)
    return jnp.swapaxes(solved, 1, 2)


def slot_index(col_codes):
    height, across_devices = (col_codes.shape[0], col_codes.shape[1])
    row_pos = jnp.arange(height, dtype=jnp.int32)[:, None, None] + col_codes // 3
    col_pos = jnp.arange(across_devices, dtype=jnp.int32)[None, :, None] + col_codes % 3
    return (row_pos * (across_devices + 2) + col_pos).reshape(-1)


def pick_rows(padded, flat_index, height, across_devices):
    features = padded.shape[2]
    flat = padded.reshape(padded.shape[0] * padded.shape[1], features)
    picked = jnp.take(flat, flat_index, axis=0)
    return picked.reshape(height, across_devices, KS, features)


def fit_slots(slot_coefficient, slot_ids, per_owner):
    members = (slot_ids[None, :] == jnp.arange(per_owner, dtype=jnp.int32)[:, None]).astype(
        jnp.float32
    )
    counts = jnp.sum(members, axis=1)
    summed = jnp.dot(
        members,
        slot_coefficient.reshape(slot_coefficient.shape[0], NC * NV),
        precision=FULL_PRECISION,
    )
    coarse = summed.reshape(per_owner, NC, NV) / jnp.maximum(counts, 1.0)[:, None, None]
    maps = solve_maps(coarse)
    return jnp.dot(members.T, maps.reshape(per_owner, NV * NC), precision=FULL_PRECISION)


def pack_slots(chosen_f, payload, group_list, capacity):
    flat = payload.reshape(group_list, capacity * payload.shape[1])
    packed = jnp.dot(chosen_f, flat, precision=FULL_PRECISION)
    return packed.reshape(chosen_f.shape[0], capacity, payload.shape[1])


def unpack_slots(chosen_f, received, block_rows):
    flat = received.reshape(received.shape[0], received.shape[1] * received.shape[2])
    return jnp.dot(chosen_f.T, flat, precision=FULL_PRECISION).reshape(
        block_rows, received.shape[2]
    )


def send_owner(payload, slot_ids):
    arrived, arrived_ids = (
        lax.all_to_all(payload, ("slab", "pencil"), split_axis=0, concat_axis=0, tiled=True),
        lax.all_to_all(slot_ids, ("slab", "pencil"), split_axis=0, concat_axis=0, tiled=True),
    )
    return (arrived, arrived_ids)


def send_back(payload):
    returned = lax.all_to_all(payload, ("slab", "pencil"), split_axis=0, concat_axis=0, tiled=True)
    return returned


def shards(a_blocks, col_codes, agg_of, test_vectors):
    height, across_devices = (agg_of.shape[0], agg_of.shape[1])
    n_slab = lax.axis_size("slab")
    n_pencil = lax.axis_size("pencil")
    devices = n_slab * n_pencil
    blocks = a_blocks.reshape(height, across_devices, KS, BLK, BLK)
    diagonal = jnp.diagonal(blocks[:, :, 0], axis1=-2, axis2=-1)
    block_wide = jnp.transpose(blocks, (0, 1, 3, 2, 4)).reshape(
        height, across_devices, BLK, KS * BLK
    )
    flat_index = slot_index(col_codes)
    candidate_vectors = test_vectors.reshape(height, across_devices, BLK, NV)
    for sweep in range(ITERS):
        padded = with_halo(
            candidate_vectors.reshape(height, across_devices, BLK * NV),
            (("slab", 0), ("pencil", 1)),
            1,
        )
        picked = pick_rows(padded, flat_index, height, across_devices).reshape(
            height, across_devices, KS * BLK, NV
        )
        image = jnp.einsum("ijor,ijrw->ijow", block_wide, picked, precision=FULL_PRECISION)
        candidate_vectors = candidate_vectors - OMEGA * image / diagonal[:, :, :, None]
    squares = jnp.sum(candidate_vectors * candidate_vectors, axis=(0, 1, 2))
    totals = lax.psum(squares, ("slab", "pencil"))
    scale = jnp.sqrt(totals / (height * across_devices * BLK * devices) + 1e-06)
    relaxed = candidate_vectors / scale
    block_rows = height * across_devices
    capacity = 2 * block_rows // devices
    group_list = devices // 2
    per_owner = block_rows // 8
    near_null_modes = coarse_modes(BLK, NC)
    row_vectors = relaxed.reshape(block_rows, BLK, NV)
    group_agg = agg_of.reshape(group_list, capacity)
    group_owner = group_agg[:, 0] // per_owner
    chosen = group_owner[None, :] == jnp.arange(devices, dtype=jnp.int32)[:, None]
    chosen_f = chosen.astype(jnp.float32)
    slot_ids = (
        jnp.sum(jnp.where(chosen[:, :, None], group_agg[None] % per_owner + 1, 0), axis=1) - 1
    )
    slot_count = devices * capacity
    outgoing = pack_slots(chosen_f, row_vectors.reshape(block_rows, BLK * NV), group_list, capacity)
    arrived, arrived_ids = send_owner(outgoing, slot_ids)
    slot_vector_rows = arrived.reshape(slot_count, BLK, NV)
    slot_coefficient = jnp.einsum(
        "wd,xwf->xdf", near_null_modes, slot_vector_rows, precision=FULL_PRECISION
    )
    slot_maps = fit_slots(slot_coefficient, arrived_ids.reshape(slot_count), per_owner)
    slot_tiles = jnp.einsum(
        "scv,svk->sck",
        slot_vector_rows,
        slot_maps.reshape(slot_count, NV, NC),
        precision=FULL_PRECISION,
    )
    returned = send_back(slot_tiles.reshape(devices, capacity, BLK * NC))
    tile_rows = unpack_slots(chosen_f, returned, block_rows).reshape(block_rows, BLK, NC)
    tile_grid = tile_rows.reshape(height, across_devices, BLK * NC)
    padded_tiles = with_halo(tile_grid, (("slab", 0), ("pencil", 1)), 1)
    picked_tiles = pick_rows(padded_tiles, flat_index, height, across_devices).reshape(
        height, across_devices, KS, BLK, NC
    )
    products = jnp.einsum("ijkoc,ijkcw->ijkow", blocks, picked_tiles, precision=FULL_PRECISION)
    return (
        relaxed.reshape(height, across_devices, BLK * NV),
        tile_grid,
        products.reshape(height, across_devices, KS * BLK * NC),
    )


def solution(mesh):
    in_specs = (
        P("slab", "pencil", None),
        P("slab", "pencil", None),
        P("slab", "pencil"),
        P("slab", "pencil", None),
    )
    out_specs = (P("slab", "pencil", None), P("slab", "pencil", None), P("slab", "pencil", None))
    return jax.shard_map(shards, mesh=mesh, in_specs=in_specs, out_specs=out_specs, check_vma=False)
```

profile of v0, /device:TPU:7, one launch (start us, length us, event | category | flops | bytes accessed | tf_op | source)
XLA Modules:
  0.0 639.7 jit_solution(15918062208513373529)
XLA Ops:
  11.9 38.9 %copy.177 = f32[16,8,20480]{0,1,2:T(8,128)} copy(f32[16,8,20480]{2,1,0:T(8,128)} %param.6) | data formatting | bytes 20971520 | tf_op args[0]
  50.9 11.6 %slice_bitcast_fusion = f32[16,8,64,64]{0,1,3,2:T(8,128)} fusion(f32[16,8,5,64,64]{0,1,4,3,2:T(8,128)} %bitcast), kind=kLoop, calls=%fused_computation.6 | loop fusion | bytes 4194304 | tf_op jit(solution)/shard_map/squeeze | solution.py:111
  76.0 6.4 %gather_fusion = f32[64,16,8]{1,2,0:T(8,128)S(1)} fusion(f32[16,8,64,64]{0,1,3,2:T(8,128)} %slice_bitcast_fusion, s32[64]{0:T(128)S(1)} %or_bitcast_fusion), kind=kCustom, calls=%fused_computation.2 | custom fusion | bytes 66048 | tf_op jit(solution)/shard_map/jit(diagonal)/gather | solution.py:111
  82.6 63.1 %copy.178 = f32[16,8,64,5,64]{2,4,3,1,0:T(8,128)} copy(f32[16,8,64,5,64]{0,1,4,2,3:T(8,128)} %bitcast.1) | data formatting | bytes 20971520 | tf_op jit(solution)/shard_map/transpose | solution.py:112
  159.8 13.7 %reshape_reshape.7 = f32[16,8,320,32]{3,2,1,0:T(8,128)} reshape(f32[640,2048]{1,0:T(8,128)} %broadcast_select_fusion.1) | data formatting | bytes 10485760 | tf_op jit(solution)/shard_map/reshape;reshape | solution.py:123
  173.5 37.9 %bitcast_subtract_fusion.1 = f32[16,8,64,32]{2,3,1,0:T(8,128)S(1)} fusion(f32[16,8,64,32]{2,3,1,0:T(8,128)} %copy.182, f32[16,8,320,32]{3,2,1,0:T(8,128)} %reshape_reshape.7, f32[16,8,64,320]{2,3,1,0:T(8,128)} %bitcast.82, f32[16,8,64]{2,1,0:T(8,128)S(1)} %copy.181), kind=kOutput, calls=%fused_computation.13 | convolution fusion | flops 1007419392 | bytes 17858560 | tf_op jit(solution)/shard_map/ijor,ijrw->ijow/dot_general | solution.py:126
  231.6 10.5 %all-to-all-start.1 = ((s32[128,1,2]{2,1,0:T(1,128)}), s32[128,1,2]{2,1,0:T(1,128)S(1)}, u32[]{:S(2)}, u32[]{:S(2)}) async-start(s32[128,1,2]{2,1,0:T(1,128)} %copy.196), calls=%async_computation.1 | async-start | bytes 131072 | tf_op jit(solution)/shard_map/all_to_all | solution.py:95
  255.5 13.8 %reshape_reshape.8 = f32[16,8,320,32]{3,2,1,0:T(8,128)} reshape(f32[640,2048]{1,0:T(8,128)} %broadcast_select_fusion) | data formatting | bytes 10485760 | tf_op jit(solution)/shard_map/reshape;reshape | solution.py:123
  269.3 38.3 %multiply_reduce_fusion = (f32[32]{0:T(128)S(1)}, f32[16,8,64,32]{2,3,1,0:T(8,128)}) fusion(f32[16,8,64,32]{2,3,1,0:T(8,128)S(1)} %copy-done.1, f32[16,8,64]{2,1,0:T(8,128)S(1)} %copy.181, f32[16,8,320,32]{3,2,1,0:T(8,128)} %reshape_reshape.8, f32[16,8,64,320]{2,3,1,0:T(8,128)} %bitcast.83), kind=kOutput, calls=%fused_computation.14 | convolution fusion | flops 1007943680 | bytes 17858688 | tf_op jit(solution)/shard_map/ijor,ijrw->ijow/dot_general | solution.py:126
  307.6 65.2 %psum.7 = f32[32]{0:T(128)S(1)} all-reduce(f32[32]{0:T(128)S(1)} %get-tuple-element.33), channel_id=1, replica_groups=mesh['slab'=16,'pencil'=8] {'slab','pencil'}, use_global_device_ids=true, to_apply=%region_1.3 | all-reduce | flops 32 | bytes 256 | tf_op jit(solution)/shard_map/psum | solution.py:129
  385.2 7.3 %all-to-all-start = ((f32[128,2,2048]{2,1,0:T(2,128)}), f32[128,2,2048]{2,1,0:T(2,128)S(1)}, u32[]{:S(2)}, u32[]{:S(2)}) async-start(f32[128,2,2048]{2,1,0:T(2,128)} %copy.192), calls=%async_computation | async-start | bytes 4194304 | tf_op jit(solution)/shard_map/all_to_all | solution.py:94
  394.1 26.8 %all-to-all-done = f32[128,2,2048]{2,1,0:T(2,128)S(1)} async-done(((f32[128,2,2048]{2,1,0:T(2,128)}), f32[128,2,2048]{2,1,0:T(2,128)S(1)}, u32[]{:S(2)}, u32[]{:S(2)}) %all-to-all-start) | async-done | bytes 2097184 | tf_op jit(solution)/shard_map/all_to_all | solution.py:94
  426.3 7.0 %copy.197 = f32[256,64,32]{0,1,2:T(8,128)S(1)} copy(f32[256,64,32]{2,1,0:T(8,128)} %reshape.246) | data formatting | bytes 4194304 | tf_op jit(solution)/shard_map/reshape | solution.py:148
  435.6 11.7 %custom-call.11 = f32[16,8,8]{2,1,0:T(8,128)S(1)} custom-call(f32[16,8,8]{2,1,0:T(8,128)S(1)} %fusion.18), custom_call_target="Cholesky" | custom-call | tf_op jit(solution)/shard_map/jit(cholesky)/cholesky | solution.py:44
  447.6 10.0 %custom-call.12 = f32[16,1,8,8]{2,3,1,0:T(8,128)S(1)} custom-call(f32[16,1,8,8]{3,2,1,0:T(8,128)S(1)} %select_bitcast_fusion), custom_call_target="InvertDiagBlocksLowerTriangular" | custom-call | tf_op jit(solution)/shard_map/jit(_solve_triangular)/vmap()/triangular_solve | solution.py:46
  459.0 11.2 %fusion.56 = f32[256,64,8]{2,1,0:T(8,128)} fusion(f32[256,64,32]{2,1,0:T(8,128)} %reshape.246, f32[256,32,8]{1,2,0:T(8,128)S(1)} %copy.209), kind=kOutput, calls=%fused_computation.114 | convolution fusion | flops 50331648 | bytes 2883584 | tf_op jit(solution)/shard_map/scv,svk->sck/dot_general | solution.py:153
  470.2 7.4 %reshape.249 = f32[128,2,512]{2,1,0:T(2,128)} reshape(f32[256,64,8]{2,1,0:T(8,128)} %fusion.56) | data formatting | bytes 1048576 | tf_op jit(solution)/shard_map/reshape | solution.py:159
  477.6 6.3 all-to-all-start.2
  484.1 11.8 %all-to-all-done.2 = f32[128,2,512]{2,1,0:T(2,128)S(1)} async-done(((f32[128,2,512]{2,1,0:T(2,128)}), f32[128,2,512]{2,1,0:T(2,128)S(1)}, u32[]{:S(2)}, u32[]{:S(2)}) %all-to-all-start.2) | async-done | bytes 524320 | tf_op jit(solution)/shard_map/all_to_all | solution.py:101
  512.7 55.6 %copy.214 = f32[16,8,5,64,64]{4,3,2,1,0:T(8,128)} copy(f32[16,8,5,64,64]{0,1,4,3,2:T(8,128)} %bitcast) | data formatting | bytes 20971520 | tf_op jit(solution)/shard_map/reshape | solution.py:110
  575.2 13.6 %gather.15 = f32[16,8,5,64,8]{4,3,2,1,0:T(8,128)} reshape(f32[640,512]{1,0:T(8,128)S(1)} %gather_fusion.1) | data formatting | bytes 2621440 | tf_op jit(solution)/shard_map/jit(_take)/gather | solution.py:60
  588.8 37.9 %fusion.4 = f32[16,8,5,64,8]{3,4,2,1,0:T(8,128)S(1)} fusion(f32[16,8,5,64,64]{4,3,2,1,0:T(8,128)} %copy.214, f32[16,8,5,64,8]{4,3,2,1,0:T(8,128)} %gather.15, pred[16,8,5]{2,1,0:T(8,128)(4,1)S(1)} %copy.211), kind=kOutput, calls=%fused_computation.16 | convolution fusion | flops 251985920 | bytes 13107840 | tf_op jit(solution)/shard_map/ijkoc,ijkcw->ijkow/dot_general | solution.py:166
  626.7 6.0 copy.215
  632.7 6.8 %copy.216 = f32[16,8,2560]{2,1,0:T(8,128)} copy(f32[16,8,2560]{0,2,1:T(8,128)} %bitcast.84) | data formatting | bytes 2621440
  (136 shorter events, 119.4 us)
Async XLA Ops:
  1.6 61.6 %collective-permute-start.1 = (f32[1,8,2048]{2,0,1:T(1,128)S(1)}, f32[1,8,2048]{2,0,1:T(1,128)S(1)}, u32[]{:S(2)}, u32[]{:S(2)}) collective-permute-start(f32[1,8,2048]{2,0,1:T(1,128)S(1)} %copy.174), channel_id=1, source_target_pairs={{8,0},{16,8},{24,16},{32,24},{40,32},{48,40},{56,48},{64,56},{72,6... | collective-permute-start | bytes 196616 | tf_op jit(solution)/shard_map/ppermute | solution.py:26
  4.1 59.0 %collective-permute-start = (f32[1,8,2048]{2,0,1:T(1,128)S(1)}, f32[1,8,2048]{2,0,1:T(1,128)S(1)}, u32[]{:S(2)}, u32[]{:S(2)}) collective-permute-start(f32[1,8,2048]{2,0,1:T(1,128)S(1)} %copy.173), channel_id=1, source_target_pairs={{0,8},{8,16},{16,24},{24,32},{32,40},{40,48},{48,56},{56,64},{64,7... | collective-permute-start | bytes 196616 | tf_op jit(solution)/shard_map/ppermute | solution.py:24
  11.6 39.3 %copy-start.4 = (s32[16,8,5]{2,1,0:T(8,128)}, s32[16,8,5]{2,1,0:T(8,128)S(1)}, u32[]{:S(2)}) copy-start(s32[16,8,5]{2,1,0:T(8,128)S(1)} %copy.172) | copy-start | bytes 7684
  11.9 39.0 %copy-start.7 = (s32[64]{0:T(128)}, s32[64]{0:T(128)S(1)}, u32[]{:S(2)}) copy-start(s32[64]{0:T(128)S(1)} %and_select_fusion.1) | copy-start | bytes 772
  50.9 11.7 %copy-start.2 = (f32[16,8,2048]{2,1,0:T(8,128)S(1)}, f32[16,8,2048]{2,1,0:T(8,128)}, u32[]{:S(2)}) copy-start(f32[16,8,2048]{2,1,0:T(8,128)} %param.9) | copy-start | bytes 3145732
  63.2 82.5 %collective-permute-start.2 = (f32[18,1,2048]{2,0,1:T(8,128)S(1)}, f32[18,1,2048]{2,0,1:T(8,128)S(1)}, u32[]{:S(2)}, u32[]{:S(2)}) collective-permute-start(f32[18,1,2048]{2,0,1:T(8,128)S(1)} %get-tuple-element.25), channel_id=1, source_target_pairs={{0,1},{1,2},{2,3},{3,4},{4,5},{5,6},{6,7},{8,9},{9,10},{10,11},{11... | collective-permute-start | bytes 442376 | tf_op jit(solution)/shard_map/ppermute | solution.py:24
  67.6 78.2 %collective-permute-start.3 = (f32[18,1,2048]{2,0,1:T(8,128)S(1)}, f32[18,1,2048]{2,0,1:T(8,128)S(1)}, u32[]{:S(2)}, u32[]{:S(2)}) collective-permute-start(f32[18,1,2048]{2,0,1:T(8,128)S(1)} %get-tuple-element.26), channel_id=1, source_target_pairs={{1,0},{2,1},{3,2},{4,3},{5,4},{6,5},{7,6},{9,8},{10,9},{11,10},{12... | collective-permute-start | bytes 442376 | tf_op jit(solution)/shard_map/ppermute | solution.py:26
  211.4 5.2 copy-start
  211.7 12.2 %collective-permute-start.4 = (f32[1,8,2048]{2,1,0:T(8,128)S(1)}, f32[1,8,2048]{2,1,0:T(8,128)S(1)}, u32[]{:S(2)}, u32[]{:S(2)}) collective-permute-start(f32[1,8,2048]{2,1,0:T(8,128)S(1)} %slice.78), channel_id=1, source_target_pairs={{0,8},{8,16},{16,24},{24,32},{32,40},{40,48},{48,56},{56,64},{64,7... | collective-permute-start | bytes 196616 | tf_op jit(solution)/shard_map/ppermute | solution.py:24
  216.8 7.1 %collective-permute-start.5 = (f32[1,8,2048]{2,1,0:T(8,128)S(1)}, f32[1,8,2048]{2,1,0:T(8,128)S(1)}, u32[]{:S(2)}, u32[]{:S(2)}) collective-permute-start(f32[1,8,2048]{2,1,0:T(8,128)S(1)} %slice.80), channel_id=1, source_target_pairs={{8,0},{16,8},{24,16},{32,24},{40,32},{48,40},{56,48},{64,56},{72,6... | collective-permute-start | bytes 196616 | tf_op jit(solution)/shard_map/ppermute | solution.py:26
  224.2 18.0 %collective-permute-start.6 = (f32[18,1,2048]{2,1,0:T(1,128)S(1)}, f32[18,1,2048]{2,1,0:T(1,128)S(1)}, u32[]{:S(2)}, u32[]{:S(2)}) collective-permute-start(f32[18,1,2048]{2,1,0:T(1,128)S(1)} %get-tuple-element.23), channel_id=1, source_target_pairs={{0,1},{1,2},{2,3},{3,4},{4,5},{5,6},{6,7},{8,9},{9,10},{10,11},{11... | collective-permute-start | bytes 442376 | tf_op jit(solution)/shard_map/ppermute | solution.py:24
  228.9 13.2 %collective-permute-start.7 = (f32[18,1,2048]{2,1,0:T(1,128)S(1)}, f32[18,1,2048]{2,1,0:T(1,128)S(1)}, u32[]{:S(2)}, u32[]{:S(2)}) collective-permute-start(f32[18,1,2048]{2,1,0:T(1,128)S(1)} %get-tuple-element.24), channel_id=1, source_target_pairs={{1,0},{2,1},{3,2},{4,3},{5,4},{6,5},{7,6},{9,8},{10,9},{11,10},{12... | collective-permute-start | bytes 442376 | tf_op jit(solution)/shard_map/ppermute | solution.py:26
  231.6 153.6 %all-to-all-start.1 = ((s32[128,1,2]{2,1,0:T(1,128)}), s32[128,1,2]{2,1,0:T(1,128)S(1)}, u32[]{:S(2)}, u32[]{:S(2)}) async-start(s32[128,1,2]{2,1,0:T(1,128)} %copy.196), calls=%async_computation.1 | async-start | bytes 131072 | tf_op jit(solution)/shard_map/all_to_all | solution.py:95
  255.5 13.8 %copy-start.1 = (f32[16,8,64,32]{2,3,1,0:T(8,128)S(1)}, f32[16,8,64,32]{2,3,1,0:T(8,128)}, u32[]{:S(2)}) copy-start(f32[16,8,64,32]{2,3,1,0:T(8,128)} %copy-done) | copy-start | bytes 3145732
  377.6 3.5 copy-start.8
  385.2 35.8 %all-to-all-start = ((f32[128,2,2048]{2,1,0:T(2,128)}), f32[128,2,2048]{2,1,0:T(2,128)S(1)}, u32[]{:S(2)}, u32[]{:S(2)}) async-start(f32[128,2,2048]{2,1,0:T(2,128)} %copy.192), calls=%async_computation | async-start | bytes 4194304 | tf_op jit(solution)/shard_map/all_to_all | solution.py:94
  470.2 13.7 %copy-start.5 = (s32[16,8,5]{2,1,0:T(8,128)S(1)}, s32[16,8,5]{2,1,0:T(8,128)}, u32[]{:S(2)}) copy-start(s32[16,8,5]{2,1,0:T(8,128)} %copy-done.4) | copy-start | bytes 7684
  477.6 18.3 %all-to-all-start.2 = ((f32[128,2,512]{2,1,0:T(2,128)}), f32[128,2,512]{2,1,0:T(2,128)S(1)}, u32[]{:S(2)}, u32[]{:S(2)}) async-start(f32[128,2,512]{2,1,0:T(2,128)} %reshape.249), calls=%async_computation.2 | async-start | bytes 1048576 | tf_op jit(solution)/shard_map/all_to_all | solution.py:101
  496.3 5.8 collective-permute-start.8
  500.1 68.1 %copy-start.3 = (f32[16,8,512]{2,1,0:T(8,128)}, f32[16,8,512]{2,1,0:T(8,128)S(1)}, u32[]{:S(2)}) copy-start(f32[16,8,512]{2,1,0:T(8,128)S(1)} %reshape_reshape_reshape.7) | copy-start | bytes 786436
  500.2 6.6 %collective-permute-start.9 = (f32[1,8,512]{2,1,0:T(8,128)S(1)}, f32[1,8,512]{2,1,0:T(8,128)S(1)}, u32[]{:S(2)}, u32[]{:S(2)}) collective-permute-start(f32[1,8,512]{2,1,0:T(8,128)S(1)} %slice.87), channel_id=1, source_target_pairs={{8,0},{16,8},{24,16},{32,24},{40,32},{48,40},{56,48},{64,56},{72,6... | collective-permute-start | bytes 49160 | tf_op jit(solution)/shard_map/ppermute | solution.py:26
  506.8 66.1 %collective-permute-start.10 = (f32[18,1,512]{2,1,0:T(1,128)S(1)}, f32[18,1,512]{2,1,0:T(1,128)S(1)}, u32[]{:S(2)}, u32[]{:S(2)}) collective-permute-start(f32[18,1,512]{2,1,0:T(1,128)S(1)} %get-tuple-element.29), channel_id=1, source_target_pairs={{0,1},{1,2},{2,3},{3,4},{4,5},{5,6},{6,7},{8,9},{9,10},{10,11},{11... | collective-permute-start | bytes 110600 | tf_op jit(solution)/shard_map/ppermute | solution.py:24
  509.9 63.0 %collective-permute-start.11 = (f32[18,1,512]{2,1,0:T(1,128)S(1)}, f32[18,1,512]{2,1,0:T(1,128)S(1)}, u32[]{:S(2)}, u32[]{:S(2)}) collective-permute-start(f32[18,1,512]{2,1,0:T(1,128)S(1)} %get-tuple-element.30), channel_id=1, source_target_pairs={{1,0},{2,1},{3,2},{4,3},{5,4},{6,5},{7,6},{9,8},{10,9},{11,10},{12... | collective-permute-start | bytes 110600 | tf_op jit(solution)/shard_map/ppermute | solution.py:26
  512.7 55.6 %copy-start.6 = (pred[16,8,5]{0,1,2:T(8,128)(4,1)S(1)}, pred[16,8,5]{0,1,2:T(8,128)(4,1)}, u32[]{:S(2)}) copy-start(pred[16,8,5]{0,1,2:T(8,128)(4,1)} %get-tuple-element.19) | copy-start | bytes 1924
where the time goes:
time: 651 us; the launch traced here: 640 us
  local copies, waits for them, and re-layouts  300 us (46%)
  matrix products  130 us (20%)
  blocking collectives  65.2 us (10%)
  starting transfers between devices  61.2 us (9%)
  waiting for transfers between devices  43.2 us (7%)
  other arithmetic  39.2 us (6%)
    dot_general x2, matrix products, shards(): jnp.einsum('ijor,ijrw->ijow', block_wide, picked, precision=FULL_PRECISION)  76.2 us
    psum x1, blocking collectives, shards(): totals = lax.psum(squares, ('slab', 'pencil'))  65.2 us
    transpose x1, local copies, waits for them, and re-layouts, shards(): jnp.transpose(blocks, (0, 1, 3, 2, 4))  63.1 us
    reshape x1, local copies, waits for them, and re-layouts, shards(): blocks = a_blocks.reshape(height, across_devices, KS, BLK, BLK)  55.6 us
    unnamed x27, local copies, waits for them, and re-layouts  47.3 us
    dot_general x1, matrix products, shards(): jnp.einsum('ijkoc,ijkcw->ijkow', blocks, picked_tiles, precision=FULL_PRE...  37.9 us
    another operation x2, local copies, waits for them, and re-layouts, shards(): pick_rows(padded, flat_index, height, across_devices)  27.5 us
    all_to_all x1, waiting for transfers between devices, send_owner(): lax.all_to_all(payload, ('slab', 'pencil'), split_axis=0, concat_axis=0,...  26.8 us
  transfers between devices with their start and end apart: 15, of which 3 were waited for; matrix products, arithmetic and copies ran while one was open for 43% of the time, Pallas kernels for 0%

commit v1 on v0

--- a/solution.py
+++ b/solution.py
@@ -126,7 +126,9 @@
         image = jnp.einsum("ijor,ijrw->ijow", block_wide, picked, precision=FULL_PRECISION)
         candidate_vectors = candidate_vectors - OMEGA * image / diagonal[:, :, :, None]
     squares = jnp.sum(candidate_vectors * candidate_vectors, axis=(0, 1, 2))
-    totals = lax.psum(squares, ("slab", "pencil"))
+    totals = squares
+    for name in ("pencil", "slab"):
+        totals = lax.psum(totals, name)
     scale = jnp.sqrt(totals / (height * across_devices * BLK * devices) + 1e-06)
     relaxed = candidate_vectors / scale
     block_rows = height * across_devices

time: 651 us -> 639 us (0.982)
  blocking collectives: 65.2 us -> 38 us
  starting transfers between devices: 61.2 us -> 76.4 us
    psum x1 -> x2, blocking collectives: 65.2 us -> 38 us  [shards(): totals = lax.psum(totals, name)]
    all_to_all x1, starting transfers between devices: 7.26 us -> 22.3 us  [send_owner(): lax.all_to_all(payload, ('slab', 'pencil'), split_axis=0, concat_axis=0,...]
  transfers between devices with their start and end apart: 15 -> 15, of which waited for: 3 -> 3; matrix products, arithmetic and copies ran while one was open for 43% -> 44% of each run, Pallas kernels for 0% -> 0%
where the time goes in v1:
time: 639 us; the launch traced here: 628 us
  local copies, waits for them, and re-layouts  300 us (47%)
  matrix products  129 us (20%)
  starting transfers between devices  76.4 us (12%)
  waiting for transfers between devices  43.3 us (7%)
  other arithmetic  39.3 us (6%)
  blocking collectives  38 us (6%)
    dot_general x2, matrix products, shards(): jnp.einsum('ijor,ijrw->ijow', block_wide, picked, precision=FULL_PRECISION)  75.9 us
    transpose x1, local copies, waits for them, and re-layouts, shards(): jnp.transpose(blocks, (0, 1, 3, 2, 4))  63.1 us
    reshape x1, local copies, waits for them, and re-layouts, shards(): blocks = a_blocks.reshape(height, across_devices, KS, BLK, BLK)  55.7 us
    unnamed x27, local copies, waits for them, and re-layouts  47.3 us
    psum x2, blocking collectives, shards(): totals = lax.psum(totals, name)  38 us
    dot_general x1, matrix products, shards(): jnp.einsum('ijkoc,ijkcw->ijkow', blocks, picked_tiles, precision=FULL_PRE...  37.9 us
    another operation x2, local copies, waits for them, and re-layouts, shards(): pick_rows(padded, flat_index, height, across_devices)  27.5 us
    all_to_all x1, waiting for transfers between devices, send_owner(): lax.all_to_all(payload, ('slab', 'pencil'), split_axis=0, concat_axis=0,...  26.9 us
  transfers between devices with their start and end apart: 15, of which 3 were waited for; matrix products, arithmetic and copies ran while one was open for 44% of the time, Pallas kernels for 0%

profile of v1, /device:TPU:7, one launch (start us, length us, event | category | flops | bytes accessed | tf_op | source)
XLA Modules:
  0.0 627.7 jit_solution(1579738094764714344)
XLA Ops:
  11.9 38.9 %copy.177 = f32[16,8,20480]{0,1,2:T(8,128)} copy(f32[16,8,20480]{2,1,0:T(8,128)} %param.6) | data formatting | bytes 20971520 | tf_op args[0]
  50.9 11.6 %slice_bitcast_fusion = f32[16,8,64,64]{0,1,3,2:T(8,128)} fusion(f32[16,8,5,64,64]{0,1,4,3,2:T(8,128)} %bitcast), kind=kLoop, calls=%fused_computation.6 | loop fusion | bytes 4194304 | tf_op jit(solution)/shard_map/squeeze | solution.py:111
  76.0 6.4 %gather_fusion = f32[64,16,8]{1,2,0:T(8,128)S(1)} fusion(f32[16,8,64,64]{0,1,3,2:T(8,128)} %slice_bitcast_fusion, s32[64]{0:T(128)S(1)} %or_bitcast_fusion), kind=kCustom, calls=%fused_computation.2 | custom fusion | bytes 66048 | tf_op jit(solution)/shard_map/jit(diagonal)/gather | solution.py:111
  82.6 63.1 %copy.178 = f32[16,8,64,5,64]{2,4,3,1,0:T(8,128)} copy(f32[16,8,64,5,64]{0,1,4,2,3:T(8,128)} %bitcast.1) | data formatting | bytes 20971520 | tf_op jit(solution)/shard_map/transpose | solution.py:112
  159.8 13.7 %reshape_reshape.7 = f32[16,8,320,32]{3,2,1,0:T(8,128)} reshape(f32[640,2048]{1,0:T(8,128)} %broadcast_select_fusion.1) | data formatting | bytes 10485760 | tf_op jit(solution)/shard_map/reshape;reshape | solution.py:123
  173.5 37.6 %bitcast_subtract_fusion.1 = f32[16,8,64,32]{2,3,1,0:T(8,128)S(1)} fusion(f32[16,8,64,32]{2,3,1,0:T(8,128)} %copy.182, f32[16,8,320,32]{3,2,1,0:T(8,128)} %reshape_reshape.7, f32[16,8,64,320]{2,3,1,0:T(8,128)} %bitcast.82, f32[16,8,64]{2,1,0:T(8,128)S(1)} %copy.181), kind=kOutput, calls=%fused_computation.13 | convolution fusion | flops 1007419392 | bytes 17858560 | tf_op jit(solution)/shard_map/ijor,ijrw->ijow/dot_general | solution.py:126
  231.3 10.8 %all-to-all-start.1 = ((s32[128,1,2]{2,1,0:T(1,128)}), s32[128,1,2]{2,1,0:T(1,128)S(1)}, u32[]{:S(2)}, u32[]{:S(2)}) async-start(s32[128,1,2]{2,1,0:T(1,128)} %copy.196), calls=%async_computation.1 | async-start | bytes 131072 | tf_op jit(solution)/shard_map/all_to_all | solution.py:95
  255.4 13.8 %reshape_reshape.8 = f32[16,8,320,32]{3,2,1,0:T(8,128)} reshape(f32[640,2048]{1,0:T(8,128)} %broadcast_select_fusion) | data formatting | bytes 10485760 | tf_op jit(solution)/shard_map/reshape;reshape | solution.py:123
  269.2 38.3 %multiply_reduce_fusion = (f32[32]{0:T(128)S(1)}, f32[16,8,64,32]{2,3,1,0:T(8,128)}) fusion(f32[16,8,64,32]{2,3,1,0:T(8,128)S(1)} %copy-done.1, f32[16,8,64]{2,1,0:T(8,128)S(1)} %copy.181, f32[16,8,320,32]{3,2,1,0:T(8,128)} %reshape_reshape.8, f32[16,8,64,320]{2,3,1,0:T(8,128)} %bitcast.83), kind=kOutput, calls=%fused_computation.14 | convolution fusion | flops 1007943680 | bytes 17858688 | tf_op jit(solution)/shard_map/ijor,ijrw->ijow/dot_general | solution.py:126
  307.5 12.1 %psum.14 = f32[32]{0:T(128)S(1)} all-reduce(f32[32]{0:T(128)S(1)} %get-tuple-element.33), channel_id=1, replica_groups=mesh['slab'=16,'pencil'=8] {'pencil'}, use_global_device_ids=true, to_apply=%region_1.3 | all-reduce | flops 32 | bytes 256 | tf_op jit(solution)/shard_map/psum | solution.py:131
  319.6 25.9 %psum.15 = f32[32]{0:T(128)S(1)} all-reduce(f32[32]{0:T(128)S(1)} %psum.14), channel_id=1, replica_groups=mesh['slab'=16,'pencil'=8] {'slab'}, use_global_device_ids=true, to_apply=%region_2.4 | all-reduce | flops 32 | bytes 256 | tf_op jit(solution)/shard_map/psum | solution.py:131
  358.0 22.3 %all-to-all-start = ((f32[128,2,2048]{2,1,0:T(2,128)}), f32[128,2,2048]{2,1,0:T(2,128)S(1)}, u32[]{:S(2)}, u32[]{:S(2)}) async-start(f32[128,2,2048]{2,1,0:T(2,128)} %copy.192), calls=%async_computation | async-start | bytes 4194304 | tf_op jit(solution)/shard_map/all_to_all | solution.py:94
  381.9 26.9 %all-to-all-done = f32[128,2,2048]{2,1,0:T(2,128)S(1)} async-done(((f32[128,2,2048]{2,1,0:T(2,128)}), f32[128,2,2048]{2,1,0:T(2,128)S(1)}, u32[]{:S(2)}, u32[]{:S(2)}) %all-to-all-start) | async-done | bytes 2097184 | tf_op jit(solution)/shard_map/all_to_all | solution.py:94
  414.2 7.0 %copy.197 = f32[256,64,32]{0,1,2:T(8,128)S(1)} copy(f32[256,64,32]{2,1,0:T(8,128)} %reshape.246) | data formatting | bytes 4194304 | tf_op jit(solution)/shard_map/reshape | solution.py:150
  423.5 11.7 %custom-call.11 = f32[16,8,8]{2,1,0:T(8,128)S(1)} custom-call(f32[16,8,8]{2,1,0:T(8,128)S(1)} %fusion.18), custom_call_target="Cholesky" | custom-call | tf_op jit(solution)/shard_map/jit(cholesky)/cholesky | solution.py:44
  435.4 10.0 %custom-call.12 = f32[16,1,8,8]{2,3,1,0:T(8,128)S(1)} custom-call(f32[16,1,8,8]{3,2,1,0:T(8,128)S(1)} %select_bitcast_fusion), custom_call_target="InvertDiagBlocksLowerTriangular" | custom-call | tf_op jit(solution)/shard_map/jit(_solve_triangular)/vmap()/triangular_solve | solution.py:46
  446.9 11.2 %fusion.56 = f32[256,64,8]{2,1,0:T(8,128)} fusion(f32[256,64,32]{2,1,0:T(8,128)} %reshape.246, f32[256,32,8]{1,2,0:T(8,128)S(1)} %copy.209), kind=kOutput, calls=%fused_computation.114 | convolution fusion | flops 50331648 | bytes 2883584 | tf_op jit(solution)/shard_map/scv,svk->sck/dot_general | solution.py:155
  458.0 7.4 %reshape.249 = f32[128,2,512]{2,1,0:T(2,128)} reshape(f32[256,64,8]{2,1,0:T(8,128)} %fusion.56) | data formatting | bytes 1048576 | tf_op jit(solution)/shard_map/reshape | solution.py:161
  465.4 6.3 %all-to-all-start.2 = ((f32[128,2,512]{2,1,0:T(2,128)}), f32[128,2,512]{2,1,0:T(2,128)S(1)}, u32[]{:S(2)}, u32[]{:S(2)}) async-start(f32[128,2,512]{2,1,0:T(2,128)} %reshape.249), calls=%async_computation.2 | async-start | bytes 1048576 | tf_op jit(solution)/shard_map/all_to_all | solution.py:101
  471.9 11.8 %all-to-all-done.2 = f32[128,2,512]{2,1,0:T(2,128)S(1)} async-done(((f32[128,2,512]{2,1,0:T(2,128)}), f32[128,2,512]{2,1,0:T(2,128)S(1)}, u32[]{:S(2)}, u32[]{:S(2)}) %all-to-all-start.2) | async-done | bytes 524320 | tf_op jit(solution)/shard_map/all_to_all | solution.py:101
  500.5 55.7 %copy.214 = f32[16,8,5,64,64]{4,3,2,1,0:T(8,128)} copy(f32[16,8,5,64,64]{0,1,4,3,2:T(8,128)} %bitcast) | data formatting | bytes 20971520 | tf_op jit(solution)/shard_map/reshape | solution.py:110
  563.2 13.5 %gather.15 = f32[16,8,5,64,8]{4,3,2,1,0:T(8,128)} reshape(f32[640,512]{1,0:T(8,128)S(1)} %gather_fusion.1) | data formatting | bytes 2621440 | tf_op jit(solution)/shard_map/jit(_take)/gather | solution.py:60
  576.7 37.9 %fusion.4 = f32[16,8,5,64,8]{3,4,2,1,0:T(8,128)S(1)} fusion(f32[16,8,5,64,64]{4,3,2,1,0:T(8,128)} %copy.214, f32[16,8,5,64,8]{4,3,2,1,0:T(8,128)} %gather.15, pred[16,8,5]{2,1,0:T(8,128)(4,1)S(1)} %copy.211), kind=kOutput, calls=%fused_computation.16 | convolution fusion | flops 251985920 | bytes 13107840 | tf_op jit(solution)/shard_map/ijkoc,ijkcw->ijkow/dot_general | solution.py:168
  620.7 6.8 %copy.216 = f32[16,8,2560]{2,1,0:T(8,128)} copy(f32[16,8,2560]{0,2,1:T(8,128)} %bitcast.84) | data formatting | bytes 2621440
  (137 shorter events, 125.4 us)
Async XLA Ops:
  1.6 61.6 %collective-permute-start.1 = (f32[1,8,2048]{2,0,1:T(1,128)S(1)}, f32[1,8,2048]{2,0,1:T(1,128)S(1)}, u32[]{:S(2)}, u32[]{:S(2)}) collective-permute-start(f32[1,8,2048]{2,0,1:T(1,128)S(1)} %copy.174), channel_id=1, source_target_pairs={{8,0},{16,8},{24,16},{32,24},{40,32},{48,40},{56,48},{64,56},{72,6... | collective-permute-start | bytes 196616 | tf_op jit(solution)/shard_map/ppermute | solution.py:26
  4.1 59.0 %collective-permute-start = (f32[1,8,2048]{2,0,1:T(1,128)S(1)}, f32[1,8,2048]{2,0,1:T(1,128)S(1)}, u32[]{:S(2)}, u32[]{:S(2)}) collective-permute-start(f32[1,8,2048]{2,0,1:T(1,128)S(1)} %copy.173), channel_id=1, source_target_pairs={{0,8},{8,16},{16,24},{24,32},{32,40},{40,48},{48,56},{56,64},{64,7... | collective-permute-start | bytes 196616 | tf_op jit(solution)/shard_map/ppermute | solution.py:24
  11.6 39.3 %copy-start.4 = (s32[16,8,5]{2,1,0:T(8,128)}, s32[16,8,5]{2,1,0:T(8,128)S(1)}, u32[]{:S(2)}) copy-start(s32[16,8,5]{2,1,0:T(8,128)S(1)} %copy.172) | copy-start | bytes 7684
  11.9 39.0 %copy-start.7 = (s32[64]{0:T(128)}, s32[64]{0:T(128)S(1)}, u32[]{:S(2)}) copy-start(s32[64]{0:T(128)S(1)} %and_select_fusion.1) | copy-start | bytes 772
  50.9 11.7 %copy-start.2 = (f32[16,8,2048]{2,1,0:T(8,128)S(1)}, f32[16,8,2048]{2,1,0:T(8,128)}, u32[]{:S(2)}) copy-start(f32[16,8,2048]{2,1,0:T(8,128)} %param.9) | copy-start | bytes 3145732
  63.2 82.5 %collective-permute-start.2 = (f32[18,1,2048]{2,0,1:T(8,128)S(1)}, f32[18,1,2048]{2,0,1:T(8,128)S(1)}, u32[]{:S(2)}, u32[]{:S(2)}) collective-permute-start(f32[18,1,2048]{2,0,1:T(8,128)S(1)} %get-tuple-element.25), channel_id=1, source_target_pairs={{0,1},{1,2},{2,3},{3,4},{4,5},{5,6},{6,7},{8,9},{9,10},{10,11},{11... | collective-permute-start | bytes 442376 | tf_op jit(solution)/shard_map/ppermute | solution.py:24
  67.6 78.2 %collective-permute-start.3 = (f32[18,1,2048]{2,0,1:T(8,128)S(1)}, f32[18,1,2048]{2,0,1:T(8,128)S(1)}, u32[]{:S(2)}, u32[]{:S(2)}) collective-permute-start(f32[18,1,2048]{2,0,1:T(8,128)S(1)} %get-tuple-element.26), channel_id=1, source_target_pairs={{1,0},{2,1},{3,2},{4,3},{5,4},{6,5},{7,6},{9,8},{10,9},{11,10},{12... | collective-permute-start | bytes 442376 | tf_op jit(solution)/shard_map/ppermute | solution.py:26
  211.1 5.2 copy-start
  211.4 12.2 %collective-permute-start.4 = (f32[1,8,2048]{2,1,0:T(8,128)S(1)}, f32[1,8,2048]{2,1,0:T(8,128)S(1)}, u32[]{:S(2)}, u32[]{:S(2)}) collective-permute-start(f32[1,8,2048]{2,1,0:T(8,128)S(1)} %slice.78), channel_id=1, source_target_pairs={{0,8},{8,16},{16,24},{24,32},{32,40},{40,48},{48,56},{56,64},{64,7... | collective-permute-start | bytes 196616 | tf_op jit(solution)/shard_map/ppermute | solution.py:24
  216.5 7.1 %collective-permute-start.5 = (f32[1,8,2048]{2,1,0:T(8,128)S(1)}, f32[1,8,2048]{2,1,0:T(8,128)S(1)}, u32[]{:S(2)}, u32[]{:S(2)}) collective-permute-start(f32[1,8,2048]{2,1,0:T(8,128)S(1)} %slice.80), channel_id=1, source_target_pairs={{8,0},{16,8},{24,16},{32,24},{40,32},{48,40},{56,48},{64,56},{72,6... | collective-permute-start | bytes 196616 | tf_op jit(solution)/shard_map/ppermute | solution.py:26
  223.9 18.2 %collective-permute-start.6 = (f32[18,1,2048]{2,1,0:T(1,128)S(1)}, f32[18,1,2048]{2,1,0:T(1,128)S(1)}, u32[]{:S(2)}, u32[]{:S(2)}) collective-permute-start(f32[18,1,2048]{2,1,0:T(1,128)S(1)} %get-tuple-element.23), channel_id=1, source_target_pairs={{0,1},{1,2},{2,3},{3,4},{4,5},{5,6},{6,7},{8,9},{9,10},{10,11},{11... | collective-permute-start | bytes 442376 | tf_op jit(solution)/shard_map/ppermute | solution.py:24
  228.6 13.5 %collective-permute-start.7 = (f32[18,1,2048]{2,1,0:T(1,128)S(1)}, f32[18,1,2048]{2,1,0:T(1,128)S(1)}, u32[]{:S(2)}, u32[]{:S(2)}) collective-permute-start(f32[18,1,2048]{2,1,0:T(1,128)S(1)} %get-tuple-element.24), channel_id=1, source_target_pairs={{1,0},{2,1},{3,2},{4,3},{5,4},{6,5},{7,6},{9,8},{10,9},{11,10},{12... | collective-permute-start | bytes 442376 | tf_op jit(solution)/shard_map/ppermute | solution.py:26
  231.3 126.6 %all-to-all-start.1 = ((s32[128,1,2]{2,1,0:T(1,128)}), s32[128,1,2]{2,1,0:T(1,128)S(1)}, u32[]{:S(2)}, u32[]{:S(2)}) async-start(s32[128,1,2]{2,1,0:T(1,128)} %copy.196), calls=%async_computation.1 | async-start | bytes 131072 | tf_op jit(solution)/shard_map/all_to_all | solution.py:95
  255.4 13.8 %copy-start.1 = (f32[16,8,64,32]{2,3,1,0:T(8,128)S(1)}, f32[16,8,64,32]{2,3,1,0:T(8,128)}, u32[]{:S(2)}) copy-start(f32[16,8,64,32]{2,3,1,0:T(8,128)} %copy-done) | copy-start | bytes 3145732
  350.4 3.5 copy-start.8
  358.0 50.9 %all-to-all-start = ((f32[128,2,2048]{2,1,0:T(2,128)}), f32[128,2,2048]{2,1,0:T(2,128)S(1)}, u32[]{:S(2)}, u32[]{:S(2)}) async-start(f32[128,2,2048]{2,1,0:T(2,128)} %copy.192), calls=%async_computation | async-start | bytes 4194304 | tf_op jit(solution)/shard_map/all_to_all | solution.py:94
  458.0 13.7 %copy-start.5 = (s32[16,8,5]{2,1,0:T(8,128)S(1)}, s32[16,8,5]{2,1,0:T(8,128)}, u32[]{:S(2)}) copy-start(s32[16,8,5]{2,1,0:T(8,128)} %copy-done.4) | copy-start | bytes 7684
  465.4 18.3 %all-to-all-start.2 = ((f32[128,2,512]{2,1,0:T(2,128)}), f32[128,2,512]{2,1,0:T(2,128)S(1)}, u32[]{:S(2)}, u32[]{:S(2)}) async-start(f32[128,2,512]{2,1,0:T(2,128)} %reshape.249), calls=%async_computation.2 | async-start | bytes 1048576 | tf_op jit(solution)/shard_map/all_to_all | solution.py:101
  484.2 5.8 collective-permute-start.8
  488.0 68.2 %copy-start.3 = (f32[16,8,512]{2,1,0:T(8,128)}, f32[16,8,512]{2,1,0:T(8,128)S(1)}, u32[]{:S(2)}) copy-start(f32[16,8,512]{2,1,0:T(8,128)S(1)} %reshape_reshape_reshape.7) | copy-start | bytes 786436
  488.0 6.6 %collective-permute-start.9 = (f32[1,8,512]{2,1,0:T(8,128)S(1)}, f32[1,8,512]{2,1,0:T(8,128)S(1)}, u32[]{:S(2)}, u32[]{:S(2)}) collective-permute-start(f32[1,8,512]{2,1,0:T(8,128)S(1)} %slice.87), channel_id=1, source_target_pairs={{8,0},{16,8},{24,16},{32,24},{40,32},{48,40},{56,48},{64,56},{72,6... | collective-permute-start | bytes 49160 | tf_op jit(solution)/shard_map/ppermute | solution.py:26
  494.7 66.1 %collective-permute-start.10 = (f32[18,1,512]{2,1,0:T(1,128)S(1)}, f32[18,1,512]{2,1,0:T(1,128)S(1)}, u32[]{:S(2)}, u32[]{:S(2)}) collective-permute-start(f32[18,1,512]{2,1,0:T(1,128)S(1)} %get-tuple-element.29), channel_id=1, source_target_pairs={{0,1},{1,2},{2,3},{3,4},{4,5},{5,6},{6,7},{8,9},{9,10},{10,11},{11... | collective-permute-start | bytes 110600 | tf_op jit(solution)/shard_map/ppermute | solution.py:24
  497.8 63.0 %collective-permute-start.11 = (f32[18,1,512]{2,1,0:T(1,128)S(1)}, f32[18,1,512]{2,1,0:T(1,128)S(1)}, u32[]{:S(2)}, u32[]{:S(2)}) collective-permute-start(f32[18,1,512]{2,1,0:T(1,128)S(1)} %get-tuple-element.30), channel_id=1, source_target_pairs={{1,0},{2,1},{3,2},{4,3},{5,4},{6,5},{7,6},{9,8},{10,9},{11,10},{12... | collective-permute-start | bytes 110600 | tf_op jit(solution)/shard_map/ppermute | solution.py:26
  500.5 55.7 %copy-start.6 = (pred[16,8,5]{0,1,2:T(8,128)(4,1)S(1)}, pred[16,8,5]{0,1,2:T(8,128)(4,1)}, u32[]{:S(2)}) copy-start(pred[16,8,5]{0,1,2:T(8,128)(4,1)} %get-tuple-element.19) | copy-start | bytes 1924
